TPU v7x, 32 devices: a whole 2x2x4 slice. The times are simulated.
32 devices in a mesh: layer: 8 (over y, x, core), spec: 4 (over z).
Axes of the slice: x: 2, y: 2, z: 4, core: 2. Of those that a mesh axis runs over, the one named last changes fastest.
Arguments:
- start_lead: float32 [64], P('spec'), may hold values from 128 to 512
- start_field: float32 [64, 8, 16, 1024], P('spec', 'layer'), may hold values from -6 to 6
- diag_dual: float32 [64, 8, 16, 1024], P('spec', 'layer'), may hold values from 0.25 to 2
- coupling_dual: float32 [64, 8, 16, 1024], P('spec', 'layer'), may hold values from -5 to 5
- linear_table: float32 [10, 8, 16, 1024], P(None, 'layer'), may hold values from -0.03125 to 0.03125
- labels: int32 [64], P('spec'), may hold values from 0 to 9
- bias_dual: float32 [64], P('spec'), may hold values from -1 to 1
- kernels: float32 [8, 3, 3, 64, 64], P('layer'), may hold values from -0.25 to 0.25
Outputs:
- grad_diag: float32 [64, 8, 16, 1024], P('spec', 'layer')
- grad_coupling: float32 [64, 8, 16, 1024], P('spec', 'layer')
- grad_linear: float32 [64, 8, 16, 1024], P('spec', 'layer')
- grad_bias: float32 [64], P('spec')
- soft_max: float32 [64], P('spec')
All inputs are finite; a program needn't handle non-finite values.
Results may differ from a plain program's by a relative error of at most 0.0003.
Values sent between devices are 32-bit elements; how exact they have to be, the bound alone decides.
A program may use at most 128 MiB of HBM per device.

v0:
```python
import functools
import math

import jax
import jax.numpy as jnp
from jax import lax
from jax.experimental import pallas as pl
from jax.experimental.pallas import tpu as pltpu
from jax.sharding import PartitionSpec as P

ITERS = 4
CHUNKS = 2
LANES = 128
MESH = pl.DeviceIdType.MESH


def pair_weights(kernel):
    zero = jnp.zeros_like(kernel[0, 0])
    rows = []
    for in_pos in range(4):
        cols = []
        for tap_row in range(3):
            for out_pos in range(2):
                tap = in_pos - out_pos
                cols.append(kernel[tap_row, tap] if 0 <= tap <= 2 else zero)
        rows.append(jnp.concatenate(cols, axis=1))
    return jnp.concatenate(rows, axis=0)


def kernel_body(
    sections,
    unit_count,
    labels,
    lead0,
    start,
    diag,
    coup,
    table,
    bias,
    wf32,
    wb32,
    grad_diag,
    grad_coup,
    grad_lin,
    small,
    z,
    img,
    rec,
    send_img,
    send_scl,
    w_buf,
    back,
    xh,
    xl,
    wfh,
    wfl,
    wbh,
    wbl,
    part,
    coef,
    lead_b,
    pk,
    gath,
    s_img_s,
    s_img_r,
    s_scl_s,
    s_scl_r,
    s_pk_s,
    s_pk_r,
):
    me = lax.axis_index("layer")
    specs, rows, width = start.shape
    per = specs // CHUNKS
    num_groups = width // LANES
    half = LANES // 2
    block_rows = per * rows

    barrier = pltpu.get_barrier_semaphore()
    for hop in range(1, sections):
        peer = lax.rem(me + hop, sections)
        pl.semaphore_signal(barrier, inc=1, device_id={"layer": peer}, device_id_type=MESH)

    for src, hi, lo in ((wf32, wfh, wfl), (wb32, wbh, wbl)):
        val = src[...]
        top = val.astype(jnp.bfloat16)
        hi[...] = top
        lo[...] = (val - top.astype(jnp.float32)).astype(jnp.bfloat16)

    def img_copy(j, c):
        sl = pl.ds(c * per, per)
        return pltpu.make_async_remote_copy(
            src_ref=send_img.at[j, sl],
            dst_ref=img.at[j, sl],
            send_sem=s_img_s.at[j, c],
            recv_sem=s_img_r.at[j, c],
            device_id={"layer": lax.rem(me + 1, sections)},
            device_id_type=MESH,
        )

    def scl_copy(j, c):
        sl = pl.ds(c * per, per)
        return pltpu.make_async_remote_copy(
            src_ref=send_scl.at[j, sl],
            dst_ref=rec.at[j, sl],
            send_sem=s_scl_s.at[j, c],
            recv_sem=s_scl_r.at[j, c],
            device_id={"layer": lax.rem(me + sections - 1, sections)},
            device_id_type=MESH,
        )

    def pk_copy(j, c, hop):
        par = j % 2
        return pltpu.make_async_remote_copy(
            src_ref=pk.at[par, c],
            dst_ref=gath.at[par, c, me],
            send_sem=s_pk_s.at[par, c, hop],
            recv_sem=s_pk_r.at[par, c, hop],
            device_id={"layer": lax.rem(me + hop, sections)},
            device_id_type=MESH,
        )

    def put_shifted(s, val):
        wide = jnp.concatenate([val, jnp.zeros((rows, LANES), jnp.float32)], axis=1)
        wide = pltpu.roll(wide, half, 1)
        top = wide.astype(jnp.bfloat16)
        at = pl.ds(pl.multiple_of(s * rows, rows), rows)
        xh[at, :] = top
        xl[at, :] = (wide - top.astype(jnp.float32)).astype(jnp.bfloat16)

    def conv(hi_w, lo_w, write):
        row = lax.rem(lax.broadcasted_iota(jnp.int32, (block_rows, LANES), 0), rows)

        def step(g, carry):
            cols = pl.ds(pl.multiple_of(g * LANES, LANES), 2 * LANES)
            a_hi = xh[:, cols]
            a_lo = xl[:, cols]
            w_hi = hi_w[...]
            prod = jnp.dot(a_hi, w_hi, preferred_element_type=jnp.float32)
            prod += jnp.dot(a_lo, w_hi, preferred_element_type=jnp.float32)
            prod += jnp.dot(a_hi, lo_w[...], preferred_element_type=jnp.float32)
            above = pltpu.roll(prod[:, :LANES], 1, 0)
            below = pltpu.roll(prod[:, 2 * LANES :], block_rows - 1, 0)
            out = prod[:, LANES : 2 * LANES]
            out += jnp.where(row == 0, 0.0, above)
            out += jnp.where(row == rows - 1, 0.0, below)
            write(g, out.reshape(per, rows, LANES))
            return carry

        lax.fori_loop(0, num_groups, step, 0)

    def wide_row(k, s):
        cf = coef[k, pl.ds(s, 1), :]
        return jnp.concatenate([cf] * num_groups, axis=1)

    def forward(j, c):
        if j < ITERS - 1:

            @pl.when(me > 0)
            def _():
                scl_copy(j, c).start()

        @pl.when(me < sections - 1)
        def _():
            def write(g, out):
                send_img[j, pl.ds(c * per, per), :, pl.ds(pl.multiple_of(g * LANES, LANES), LANES)] = out

            conv(wfh, wfl, write)
            img_copy(j, c).start()

    def fold(val):
        acc = val[:, :LANES]
        for g in range(1, num_groups):
            acc = acc + val[:, g * LANES : (g + 1) * LANES]
        return jnp.sum(acc, axis=0, keepdims=True)

    def apply(j, c):
        last = j == ITERS - 1

        @pl.when(me > 0)
        def _():
            img_copy(j, c).wait_recv()

        if not last:

            @pl.when(me < sections - 1)
            def _():
                scl_copy(j, c).wait_recv()

                def shift_one(s, carry):
                    put_shifted(s, rec[j, c * per + s])
                    return carry

                lax.fori_loop(0, per, shift_one, 0)

                def write(g, out):
                    back[:, :, pl.ds(pl.multiple_of(g * LANES, LANES), LANES)] = out

                conv(wbh, wbl, write)

        coef[0] = lead_b[j, c]

        def one(s, carry):
            sp = c * per + s
            zs = z[j, sp]
            lin = table[labels[sp]]
            if last:
                w = diag[sp] * zs - coup[sp] * img[j, sp]
            else:
                w = diag[sp] * zs - 0.5 * (coup[sp] * img[j, sp] + back[s])
            w = w + lin * (0.5 * wide_row(0, s))
            part[0, pl.ds(s, 1), :] = fold(lin * zs)
            part[1, pl.ds(s, 1), :] = fold(zs * w)
            if not last:
                w_buf[sp] = w
                part[2, pl.ds(s, 1), :] = fold(w * w)
            if j == 0:
                part[3, pl.ds(s, 1), :] = fold(zs * zs)
            return carry

        lax.fori_loop(0, per, one, 0)
        lane = lax.broadcasted_iota(jnp.int32, (per, LANES), 1)
        packet = jnp.zeros((per, LANES), jnp.float32)
        for k in range(4 if j == 0 else (2 if last else 3)):
            packet = jnp.where(lane == k, jnp.sum(part[k], axis=1, keepdims=True), packet)
        pk[j % 2, c] = packet
        gath[j % 2, c, me] = packet
        for hop in range(1, sections):
            pk_copy(j, c, hop).start()

    def totals(j, c, count):
        for hop in range(1, sections):
            pk_copy(j, c, hop).wait()
        total = gath[j % 2, c, 0]
        for peer in range(1, sections):
            total = total + gath[j % 2, c, peer]
        return [jnp.broadcast_to(total[:, k : k + 1], (per, LANES)) for k in range(count)]

    @pl.when(me == 0)
    def _():
        def clear(s, carry):
            for j in range(ITERS):
                img[j, s] = jnp.zeros((rows, width), jnp.float32)
            return carry

        lax.fori_loop(0, specs, clear, 0)

    @pl.when(me == sections - 1)
    def _():
        def clear(s, carry):
            back[s] = jnp.zeros((rows, width), jnp.float32)
            return carry

        lax.fori_loop(0, per, clear, 0)

    pl.semaphore_wait(barrier, sections - 1)

    state = [{"alpha": [], "beta": []} for _ in range(CHUNKS)]
    for c in range(CHUNKS):
        lead_b[0, c] = jnp.broadcast_to(lead0[c * per : (c + 1) * per, :], (per, LANES))

        def first(s, carry):
            sp = c * per + s
            val = start[sp]
            z[0, sp] = val
            send_scl[0, sp] = coup[sp] * val
            put_shifted(s, val)
            return carry

        lax.fori_loop(0, per, first, 0)
        forward(0, c)

    for j in range(ITERS - 1):
        for c in range(CHUNKS):
            apply(j, c)
            st = state[c]
            bias_c = jnp.broadcast_to(bias[c * per : (c + 1) * per, :], (per, LANES))
            sums = totals(j, c, 4 if j == 0 else 3)
            lead_now = lead_b[j, c]
            image_lead = bias_c * lead_now + 0.5 * sums[0]
            if j == 0:
                factor = 1.0 / jnp.sqrt(lead_now * lead_now + sums[3])
                st["factor"] = factor
                alpha = factor * factor * (lead_now * image_lead + sums[1])
                lead_now = lead_now * factor
                image_lead = image_lead * factor
                power = factor * factor * sums[2]
                rest_lead = image_lead - alpha * lead_now
                beta = jnp.sqrt(image_lead * image_lead + power - alpha * alpha + 1e-06)
                inv = factor / beta
                lead_b[0, c] = lead_now
                coef[1] = inv
                coef[2] = -alpha * inv
            else:
                beta_old = st["beta"][-1]
                lead_old = lead_b[j - 1, c]
                alpha = lead_now * image_lead + sums[1]
                rest_lead = image_lead - alpha * lead_now - beta_old * lead_old
                beta = jnp.sqrt(image_lead * image_lead + sums[2] - alpha * alpha - beta_old * beta_old + 1e-06)
                inv = 1.0 / beta
                coef[1] = inv
                coef[2] = -alpha * inv
                coef[3] = -beta_old * inv * (st["factor"] if j == 1 else 1.0)
            lead_b[j + 1, c] = rest_lead / beta
            st["alpha"].append(alpha)
            st["beta"].append(beta)

            def advance(s, carry):
                sp = c * per + s
                val = w_buf[sp] * wide_row(1, s) + z[j, sp] * wide_row(2, s)
                if j > 0:
                    val = val + z[j - 1, sp] * wide_row(3, s)
                z[j + 1, sp] = val
                if j + 1 < ITERS - 1:
                    send_scl[j + 1, sp] = coup[sp] * val
                put_shifted(s, val)
                return carry

            lax.fori_loop(0, per, advance, 0)
            forward(j + 1, c)

    lane = lax.broadcasted_iota(jnp.int32, (per, LANES), 1)
    last = ITERS - 1
    for c in range(CHUNKS):
        apply(last, c)
    for c in range(CHUNKS):
        st = state[c]
        bias_c = jnp.broadcast_to(bias[c * per : (c + 1) * per, :], (per, LANES))
        sums = totals(last, c, 2)
        lead_now = lead_b[last, c]
        alpha = lead_now * (bias_c * lead_now + 0.5 * sums[0]) + sums[1]
        alphas = st["alpha"] + [alpha]
        betas = st["beta"]
        n = ITERS
        zero = jnp.zeros((per, LANES), jnp.float32)
        tri = [[zero] * n for _ in range(n)]
        norm = zero
        for i in range(n):
            tri[i][i] = alphas[i]
            norm = norm + alphas[i] * alphas[i]
            if i + 1 < n:
                tri[i][i + 1] = betas[i]
                tri[i + 1][i] = betas[i]
                norm = norm + 2.0 * (betas[i] * betas[i])
        scale = 0.5 / jnp.sqrt(norm)
        sx = [[tri[i][k] * scale for k in range(n)] for i in range(n)]
        expo = [[zero + (1.0 if i == k else 0.0) for k in range(n)] for i in range(n)]
        for degree in range(12, 0, -1):
            nxt = []
            for i in range(n):
                line = []
                for k in range(n):
                    acc = None
                    for m in range(max(0, i - 1), min(n, i + 2)):
                        term = sx[i][m] * expo[m][k]
                        acc = term if acc is None else acc + term
                    acc = acc * (1.0 / degree)
                    line.append(acc + 1.0 if i == k else acc)
                nxt.append(line)
            expo = nxt
        for _ in range(4):
            nxt = [[None] * n for _ in range(n)]
            for i in range(n):
                for k in range(n):
                    acc = expo[i][0] * expo[0][k]
                    for m in range(1, n):
                        acc = acc + expo[i][m] * expo[m][k]
                    nxt[i][k] = acc
            expo = nxt
        trace = expo[0][0] + expo[1][1] + expo[2][2] + expo[3][3]
        inv = 1.0 / trace
        wt = [[expo[i][k] * inv for k in range(n)] for i in range(n)]
        soft = zero
        gbias = zero
        leads = [lead_b[i, c] for i in range(n)]
        for i in range(n):
            for k in range(n):
                if abs(i - k) <= 1:
                    soft = soft + wt[i][k] * tri[i][k]
                gbias = gbias + wt[i][k] * (leads[i] * leads[k])
        small[c * per : (c + 1) * per, :] = jnp.where(lane == 0, gbias, soft)
        fac = [st["factor"], None, None, None]

        def scaled_by(val, *which):
            for i in which:
                if fac[i] is not None:
                    val = val * fac[i]
            return val

        slot = 0
        pair_slot = {}
        for i in range(n):
            for k in range(i, n):
                val = wt[i][k] if i == k else wt[i][k] + wt[k][i]
                coef[slot] = unit_count * scaled_by(val, i, k)
                pair_slot[i, k] = slot
                slot += 1
        mix_slot = {}
        for i in range(n):
            for k in range(n):
                coef[slot] = -unit_count * scaled_by(wt[i][k], i, k)
                mix_slot[i, k] = slot
                slot += 1
        lin_slot = {}
        for k in range(n):
            val = wt[0][k] * leads[0]
            for i in range(1, n):
                val = val + wt[i][k] * leads[i]
            coef[slot] = math.sqrt(unit_count) * scaled_by(val, k)
            lin_slot[k] = slot
            slot += 1

        def final(s, carry):
            sp = c * per + s
            cf = [coef[k, pl.ds(s, 1), :] for k in range(slot)]
            for g in range(num_groups):
                cols = slice(g * LANES, (g + 1) * LANES)
                zs = [z[i, sp, :, cols] for i in range(n)]
                ims = [img[i, sp, :, cols] for i in range(n)]
                gd = gc = gl = None
                for i in range(n):
                    mixed = zs[i] * cf[pair_slot[i, i]]
                    for k in range(i + 1, n):
                        mixed = mixed + zs[k] * cf[pair_slot[i, k]]
                    mixed_img = ims[0] * cf[mix_slot[i, 0]]
                    for k in range(1, n):
                        mixed_img = mixed_img + ims[k] * cf[mix_slot[i, k]]
                    gd = zs[i] * mixed if gd is None else gd + zs[i] * mixed
                    gc = zs[i] * mixed_img if gc is None else gc + zs[i] * mixed_img
                    lin = zs[i] * cf[lin_slot[i]]
                    gl = lin if gl is None else gl + lin
                grad_diag[sp, :, cols] = gd
                grad_coup[sp, :, cols] = gc
                grad_lin[sp, :, cols] = gl
            return carry

        lax.fori_loop(0, per, final, 0)

    @pl.when(me < sections - 1)
    def _():
        for j in range(ITERS):
            for c in range(CHUNKS):
                img_copy(j, c).wait_send()

    @pl.when(me > 0)
    def _():
        for j in range(ITERS - 1):
            for c in range(CHUNKS):
                scl_copy(j, c).wait_send()


def body(start_lead, start_field, diag_dual, coupling_dual, linear_table, labels, bias_dual, kernels):
    sections = lax.axis_size("layer")
    specs, _, rows, width = start_field.shape
    unit_count = sections * rows * width
    per = specs // CHUNKS
    kern = kernels[0]
    wf = pair_weights(kern)
    wb = pair_weights(jnp.swapaxes(kern[::-1, ::-1], 2, 3))
    shape3 = (specs, rows, width)
    full = pl.BlockSpec(memory_space=pltpu.VMEM)
    f32, bf16 = jnp.float32, jnp.bfloat16
    dma = pltpu.SemaphoreType.DMA
    outs = pl.pallas_call(
        functools.partial(kernel_body, sections, float(unit_count)),
        out_shape=[jax.ShapeDtypeStruct(shape3, f32)] * 3 + [jax.ShapeDtypeStruct((specs, LANES), f32)],
        in_specs=[pl.BlockSpec(memory_space=pltpu.SMEM)] + [full] * 8,
        out_specs=[full] * 4,
        scratch_shapes=[
            pltpu.VMEM((ITERS,) + shape3, f32),
            pltpu.VMEM((ITERS,) + shape3, f32),
            pltpu.VMEM((ITERS - 1,) + shape3, f32),
            pltpu.VMEM((ITERS,) + shape3, f32),
            pltpu.VMEM((ITERS - 1,) + shape3, f32),
            pltpu.VMEM(shape3, f32),
            pltpu.VMEM((per, rows, width), f32),
            pltpu.VMEM((per * rows, width + LANES), bf16),
            pltpu.VMEM((per * rows, width + LANES), bf16),
            pltpu.VMEM(wf.shape, bf16),
            pltpu.VMEM(wf.shape, bf16),
            pltpu.VMEM(wf.shape, bf16),
            pltpu.VMEM(wf.shape, bf16),
            pltpu.VMEM((4, per, LANES), f32),
            pltpu.VMEM((32, per, LANES), f32),
            pltpu.VMEM((ITERS, CHUNKS, per, LANES), f32),
            pltpu.VMEM((2, CHUNKS, per, LANES), f32),
            pltpu.VMEM((2, CHUNKS, sections, per, LANES), f32),
            dma((ITERS, CHUNKS)),
            dma((ITERS, CHUNKS)),
            dma((ITERS - 1, CHUNKS)),
            dma((ITERS - 1, CHUNKS)),
            dma((2, CHUNKS, sections)),
            dma((2, CHUNKS, sections)),
        ],
        compiler_params=pltpu.CompilerParams(collective_id=0, has_side_effects=True, vmem_limit_bytes=56 * 1024 * 1024),
    )(
        labels,
        start_lead[:, None],
        start_field.reshape(shape3),
        diag_dual.reshape(shape3),
        coupling_dual.reshape(shape3),
        linear_table.reshape(linear_table.shape[0], rows, width),
        bias_dual[:, None],
        wf,
        wb,
    )
    big = [out.reshape(start_field.shape) for out in outs[:3]]
    return (*big, outs[3][:, 0], outs[3][:, 1])


def solution(mesh):
    placed = (
        P("spec"),
        P("spec", "layer", None, None),
        P("spec", "layer", None, None),
        P("spec", "layer", None, None),
        P(None, "layer", None, None),
        P("spec"),
        P("spec"),
        P("layer", None, None, None, None),
    )
    return jax.shard_map(
        body,
        mesh=mesh,
        in_specs=placed,
        out_specs=(
            P("spec", "layer", None, None),
            P("spec", "layer", None, None),
            P("spec", "layer", None, None),
            P("spec"),
            P("spec"),
        ),
        check_vma=False,
    )
```

profile of v0, /device:TPU:0, one launch (start us, length us, event | category | flops | bytes accessed | tf_op | source)
XLA Modules:
  0.0 137.2 jit_solution(15243132908612407035)
XLA Ops:
  0.6 0.6 copy-done.4
  1.3 0.7 copy.48.lead0
  2.0 0.7 copy.49.bias
  2.6 1.0 reverse_bitcast_fusion
  3.8 0.1 copy.42
  4.1 0.1 copy.34
  4.3 0.1 copy.36
  4.4 0.1 concatenate.37
  4.5 0.1 concatenate.36
  4.7 0.1 concatenate.35
  4.8 0.1 concatenate.38
  4.9 0.7 copy-done
  5.6 0.1 concatenate.31
  5.7 0.1 concatenate.30
  5.8 0.1 concatenate.32
  6.0 0.1 concatenate.33
  6.1 0.9 pad_maximum_fusion
  7.0 123.8 %shard_map.119 = (f32[16,16,1024]{2,1,0:T(8,128)}, f32[16,16,1024]{2,1,0:T(8,128)}, f32[16,16,1024]{2,1,0:T(8,128)}, f32[16,128]{1,0:T(8,128)}) custom-call(s32[16]{0:T(128)} %labels.1, f32[16,1]{1,0:T(8,128)} %copy.48.lead0, f32[16,16,1024]{2,1,0:T(8,128)} %bitcast.53, f32[16,16,1024]{2,1,0:T(8,128)} %bitcast.54, f32[16,16,1024]{2,1,0:T(8,128)} %bitcast.55, ...), custom_call_target="tpu_custom_call" | custom-call | tf_op jit(solution)/shard_map/pallas_call | solution.py:463
  130.8 0.7 copy-done.3
  131.5 0.7 slice_reduce_fusion
  132.2 2.4 %copy.56 = f32[16,1,16,1024]{3,2,1,0:T(8,128)} copy(f32[16,1,16,1024]{3,2,1,0:T(8,128)} %bitcast.58) | data formatting | bytes 2097152
  134.6 1.0 copy.57
  135.6 0.6 copy-done.1
  136.2 1.0 copy.58
  (17 shorter events, 0.5 us)
Async XLA Ops:
  0.6 0.7 copy-start.4
  1.3 0.7 copy-start.5
  4.6 1.0 copy-start
  130.8 0.7 copy-start.3
  132.2 2.4 %copy-start.2 = (f32[16,16,1024]{2,1,0:T(8,128)S(1)}, f32[16,16,1024]{2,1,0:T(8,128)}, u32[]{:S(2)}) copy-start(f32[16,16,1024]{2,1,0:T(8,128)} %get-tuple-element.10) | copy-start | bytes 3145732
  134.6 1.6 %copy-start.1 = (f32[16,16,1024]{2,1,0:T(8,128)S(1)}, f32[16,16,1024]{2,1,0:T(8,128)}, u32[]{:S(2)}) copy-start(f32[16,16,1024]{2,1,0:T(8,128)} %get-tuple-element.11) | copy-start | bytes 3145732
where the time goes:
time: 137 us
  Pallas kernels  124 us (91%)
  local copies, waits for them, and re-layouts  11.7 us (9%)
    pallas_call x1, Pallas kernels, body(): pl.pallas_call(functools.partial(kernel_body, sections, float(unit_count)...  124 us
    unnamed x15, local copies, waits for them, and re-layouts  7.06 us

commit v1 on v0

--- a/solution.py
+++ b/solution.py
@@ -12,19 +12,6 @@
 CHUNKS = 2
 LANES = 128
 MESH = pl.DeviceIdType.MESH
-
-
-def pair_weights(kernel):
-    zero = jnp.zeros_like(kernel[0, 0])
-    rows = []
-    for in_pos in range(4):
-        cols = []
-        for tap_row in range(3):
-            for out_pos in range(2):
-                tap = in_pos - out_pos
-                cols.append(kernel[tap_row, tap] if 0 <= tap <= 2 else zero)
-        rows.append(jnp.concatenate(cols, axis=1))
-    return jnp.concatenate(rows, axis=0)
 
 
 def kernel_body(
@@ -37,8 +24,7 @@
     coup,
     table,
     bias,
-    wf32,
-    wb32,
+    kern,
     grad_diag,
     grad_coup,
     grad_lin,
@@ -80,11 +66,19 @@
         peer = lax.rem(me + hop, sections)
         pl.semaphore_signal(barrier, inc=1, device_id={"layer": peer}, device_id_type=MESH)
 
-    for src, hi, lo in ((wf32, wfh, wfl), (wb32, wbh, wbl)):
-        val = src[...]
-        top = val.astype(jnp.bfloat16)
-        hi[...] = top
-        lo[...] = (val - top.astype(jnp.float32)).astype(jnp.bfloat16)
+    chan = kern.shape[-1]
+    zero_tap = jnp.zeros((chan, chan), jnp.float32)
+    for tap_row in range(3):
+        fwd_taps = [kern[tap_row, tap] for tap in range(3)]
+        back_taps = [jnp.transpose(kern[2 - tap_row, 2 - tap]) for tap in range(3)]
+        for taps, hi, lo in ((fwd_taps, wfh, wfl), (back_taps, wbh, wbl)):
+            for in_pos in range(4):
+                pieces = [taps[in_pos - q] if 0 <= in_pos - q <= 2 else zero_tap for q in range(2)]
+                val = jnp.concatenate(pieces, axis=1)
+                top = val.astype(jnp.bfloat16)
+                at = (slice(in_pos * chan, (in_pos + 1) * chan), slice(tap_row * LANES, (tap_row + 1) * LANES))
+                hi[at] = top
+                lo[at] = (val - top.astype(jnp.float32)).astype(jnp.bfloat16)
 
     def img_copy(j, c):
         sl = pl.ds(c * per, per)
@@ -173,6 +167,12 @@
             acc = acc + val[:, g * LANES : (g + 1) * LANES]
         return jnp.sum(acc, axis=0, keepdims=True)
 
+    def recur(ref, val, j, sp, s):
+        val = val * wide_row(1, s) + ref[j - 1, sp] * wide_row(2, s)
+        if j > 1:
+            val = val + ref[j - 2, sp] * wide_row(3, s)
+        return val
+
     def apply(j, c):
         last = j == ITERS - 1
 
@@ -187,7 +187,11 @@
                 scl_copy(j, c).wait_recv()
 
                 def shift_one(s, carry):
-                    put_shifted(s, rec[j, c * per + s])
+                    val = rec[j, c * per + s]
+                    if j > 0:
+                        val = recur(rec, val, j, c * per + s, s)
+                        rec[j, c * per + s] = val
+                    put_shifted(s, val)
                     return carry
 
                 lax.fori_loop(0, per, shift_one, 0)
@@ -203,15 +207,22 @@
             sp = c * per + s
             zs = z[j, sp]
             lin = table[labels[sp]]
+            image = img[j, sp]
+            if j > 0:
+                image = recur(img, image, j, sp, s)
+                img[j, sp] = image
             if last:
-                w = diag[sp] * zs - coup[sp] * img[j, sp]
+                w = diag[sp] * zs - coup[sp] * image
             else:
-                w = diag[sp] * zs - 0.5 * (coup[sp] * img[j, sp] + back[s])
+                w = diag[sp] * zs - 0.5 * (coup[sp] * image + back[s])
             w = w + lin * (0.5 * wide_row(0, s))
             part[0, pl.ds(s, 1), :] = fold(lin * zs)
             part[1, pl.ds(s, 1), :] = fold(zs * w)
             if not last:
                 w_buf[sp] = w
+                put_shifted(s, w)
+                if j + 1 < ITERS - 1:
+                    send_scl[j + 1, sp] = coup[sp] * w
                 part[2, pl.ds(s, 1), :] = fold(w * w)
             if j == 0:
                 part[3, pl.ds(s, 1), :] = fold(zs * zs)
@@ -269,9 +280,11 @@
         lax.fori_loop(0, per, first, 0)
         forward(0, c)
 
+    for c in range(CHUNKS):
+        apply(0, c)
+        forward(1, c)
     for j in range(ITERS - 1):
         for c in range(CHUNKS):
-            apply(j, c)
             st = state[c]
             bias_c = jnp.broadcast_to(bias[c * per : (c + 1) * per, :], (per, LANES))
             sums = totals(j, c, 4 if j == 0 else 3)
@@ -310,18 +323,15 @@
                 if j > 0:
                     val = val + z[j - 1, sp] * wide_row(3, s)
                 z[j + 1, sp] = val
-                if j + 1 < ITERS - 1:
-                    send_scl[j + 1, sp] = coup[sp] * val
-                put_shifted(s, val)
                 return carry
 
             lax.fori_loop(0, per, advance, 0)
-            forward(j + 1, c)
+            apply(j + 1, c)
+            if j + 1 < ITERS - 1:
+                forward(j + 2, c)
 
     lane = lax.broadcasted_iota(jnp.int32, (per, LANES), 1)
     last = ITERS - 1
-    for c in range(CHUNKS):
-        apply(last, c)
     for c in range(CHUNKS):
         st = state[c]
         bias_c = jnp.broadcast_to(bias[c * per : (c + 1) * per, :], (per, LANES))
@@ -453,9 +463,7 @@
     specs, _, rows, width = start_field.shape
     unit_count = sections * rows * width
     per = specs // CHUNKS
-    kern = kernels[0]
-    wf = pair_weights(kern)
-    wb = pair_weights(jnp.swapaxes(kern[::-1, ::-1], 2, 3))
+    chan = kernels.shape[-1]
     shape3 = (specs, rows, width)
     full = pl.BlockSpec(memory_space=pltpu.VMEM)
     f32, bf16 = jnp.float32, jnp.bfloat16
@@ -463,7 +471,7 @@
     outs = pl.pallas_call(
         functools.partial(kernel_body, sections, float(unit_count)),
         out_shape=[jax.ShapeDtypeStruct(shape3, f32)] * 3 + [jax.ShapeDtypeStruct((specs, LANES), f32)],
-        in_specs=[pl.BlockSpec(memory_space=pltpu.SMEM)] + [full] * 8,
+        in_specs=[pl.BlockSpec(memory_space=pltpu.SMEM)] + [full] * 7,
         out_specs=[full] * 4,
         scratch_shapes=[
             pltpu.VMEM((ITERS,) + shape3, f32),
@@ -475,10 +483,10 @@
             pltpu.VMEM((per, rows, width), f32),
             pltpu.VMEM((per * rows, width + LANES), bf16),
             pltpu.VMEM((per * rows, width + LANES), bf16),
-            pltpu.VMEM(wf.shape, bf16),
-            pltpu.VMEM(wf.shape, bf16),
-            pltpu.VMEM(wf.shape, bf16),
-            pltpu.VMEM(wf.shape, bf16),
+            pltpu.VMEM((4 * chan, 6 * chan), bf16),
+            pltpu.VMEM((4 * chan, 6 * chan), bf16),
+            pltpu.VMEM((4 * chan, 6 * chan), bf16),
+            pltpu.VMEM((4 * chan, 6 * chan), bf16),
             pltpu.VMEM((4, per, LANES), f32),
             pltpu.VMEM((32, per, LANES), f32),
             pltpu.VMEM((ITERS, CHUNKS, per, LANES), f32),
@@ -500,8 +508,7 @@
         coupling_dual.reshape(shape3),
         linear_table.reshape(linear_table.shape[0], rows, width),
         bias_dual[:, None],
-        wf,
-        wb,
+        kernels.reshape(kernels.shape[1:]),
     )
     big = [out.reshape(start_field.shape) for out in outs[:3]]
     return (*big, outs[3][:, 0], outs[3][:, 1])

time: 137 us -> 108 us (0.79)
  Pallas kernels: 124 us -> 97.6 us
  local copies, waits for them, and re-layouts: 11.7 us -> 9.1 us
    pallas_call x1, Pallas kernels: 124 us -> 97.6 us  [body(): pl.pallas_call(functools.partial(kernel_body, sections, float(unit_count)...]
    unnamed x15 -> x11, local copies, waits for them, and re-layouts: 7.06 us -> 6.27 us
where the time goes in v1:
time: 108 us; the launch traced here: 107 us
  Pallas kernels  97.6 us (90%)
  local copies, waits for them, and re-layouts  9.1 us (8%)
    pallas_call x1, Pallas kernels, body(): pl.pallas_call(functools.partial(kernel_body, sections, float(unit_count)...  97.6 us
    unnamed x11, local copies, waits for them, and re-layouts  6.27 us

profile of v1, /device:TPU:0, one launch (start us, length us, event | category | flops | bytes accessed | tf_op | source)
XLA Modules:
  0.0 107.4 jit_solution(9127710333690290574)
XLA Ops:
  0.6 0.0 copy-start.2
  0.6 0.6 copy-done.2
  1.3 0.7 copy.18.lead0
  2.0 0.0 copy-start.3
  2.0 0.7 copy-done.3
  2.6 0.7 copy.19.bias
  3.3 97.6 %shard_map.119 = (f32[16,16,1024]{2,1,0:T(8,128)}, f32[16,16,1024]{2,1,0:T(8,128)}, f32[16,16,1024]{2,1,0:T(8,128)}, f32[16,128]{1,0:T(8,128)}) custom-call(s32[16]{0:T(128)} %labels.1, f32[16,1]{1,0:T(8,128)} %copy.18.lead0, f32[16,16,1024]{2,1,0:T(8,128)} %bitcast.19, f32[16,16,1024]{2,1,0:T(8,128)} %bitcast.20, f32[16,16,1024]{2,1,0:T(8,128)} %bitcast.21, ...), custom_call_target="tpu_custom_call" | custom-call | tf_op jit(solution)/shard_map/pallas_call | solution.py:471
  100.9 1.5 %slice_reduce_fusion = (f32[16]{0:T(128)}, f32[16]{0:T(128)}) fusion(f32[16,128]{1,0:T(8,128)} %get-tuple-element.12), kind=kLoop, calls=%fused_computation | loop fusion | bytes 256 | tf_op jit(solution)/shard_map/slice | solution.py:514
  102.4 0.0 copy-start.1
  102.4 2.4 %copy.26 = f32[16,1,16,1024]{3,2,1,0:T(8,128)} copy(f32[16,1,16,1024]{3,2,1,0:T(8,128)} %bitcast.18) | data formatting | bytes 2097152
  104.8 0.0 copy-done.1
  104.8 0.0 copy-start
  104.8 1.0 copy.27
  105.8 0.6 copy-done
  106.4 1.0 copy.28
Async XLA Ops:
  0.6 0.7 copy-start.2
  2.0 0.7 copy-start.3
  102.4 2.4 %copy-start.1 = (f32[16,16,1024]{2,1,0:T(8,128)S(1)}, f32[16,16,1024]{2,1,0:T(8,128)}, u32[]{:S(2)}) copy-start(f32[16,16,1024]{2,1,0:T(8,128)} %get-tuple-element.10) | copy-start | bytes 3145732
  104.8 1.6 %copy-start = (f32[16,16,1024]{2,1,0:T(8,128)S(1)}, f32[16,16,1024]{2,1,0:T(8,128)}, u32[]{:S(2)}) copy-start(f32[16,16,1024]{2,1,0:T(8,128)} %get-tuple-element.11) | copy-start | bytes 3145732

commit v2 on v1

--- a/solution.py
+++ b/solution.py
@@ -11,6 +11,8 @@
 ITERS = 4
 CHUNKS = 2
 LANES = 128
+RELAY_SECTIONS = 8
+IMAGES_VIA_LAST = True
 MESH = pl.DeviceIdType.MESH
 
 
@@ -53,6 +55,11 @@
     s_scl_r,
     s_pk_s,
     s_pk_r,
+    rly,
+    s_in_s,
+    s_in_r,
+    s_out_s,
+    s_out_r,
 ):
     me = lax.axis_index("layer")
     specs, rows, width = start.shape
@@ -80,8 +87,72 @@
                 hi[at] = top
                 lo[at] = (val - top.astype(jnp.float32)).astype(jnp.bfloat16)
 
-    def img_copy(j, c):
-        sl = pl.ds(c * per, per)
+    relayed = sections == RELAY_SECTIONS
+    low, high = sections // 2 - 1, sections // 2
+    img_via, scl_via = (sections - 1, 0) if IMAGES_VIA_LAST else (0, sections - 1)
+    direct = per // 2
+    near = jnp.logical_and
+
+    def relay_in(j, c, images):
+        src = send_img if images else send_scl
+        return pltpu.make_async_remote_copy(
+            src_ref=src.at[j, pl.ds(c * per + direct, per - direct)],
+            dst_ref=rly.at[j, pl.ds(c * (per - direct), per - direct)],
+            send_sem=s_in_s.at[j, c],
+            recv_sem=s_in_r.at[j, c],
+            device_id={"layer": jnp.int32(img_via if images else scl_via)},
+            device_id_type=MESH,
+        )
+
+    def relay_out(j, c, images):
+        dst = img if images else rec
+        return pltpu.make_async_remote_copy(
+            src_ref=rly.at[j, pl.ds(c * (per - direct), per - direct)],
+            dst_ref=dst.at[j, pl.ds(c * per + direct, per - direct)],
+            send_sem=s_out_s.at[j, c],
+            recv_sem=s_out_r.at[j, c],
+            device_id={"layer": jnp.int32(high if images else low)},
+            device_id_type=MESH,
+        )
+
+    def pass_on(j, c):
+        if not relayed:
+            return
+        for images, via in ((True, img_via), (False, scl_via)):
+            if images or j < ITERS - 1:
+
+                @pl.when(me == via)
+                def _():
+                    relay_in(j, c, images).wait_recv()
+                    relay_out(j, c, images).start()
+
+    def each_copy(j, c, images, side, act):
+        copy = img_copy if images else scl_copy
+        if images:
+            has = me < sections - 1 if side == 0 else me > 0
+            middle = low if side == 0 else high
+        else:
+            has = me > 0 if side == 0 else me < sections - 1
+            middle = high if side == 0 else low
+        if not relayed:
+
+            @pl.when(has)
+            def _():
+                act(copy(j, c))
+
+            return
+
+        @pl.when(near(has, me != middle))
+        def _():
+            act(copy(j, c))
+
+        @pl.when(me == middle)
+        def _():
+            act(copy(j, c, direct))
+            act(relay_in(j, c, images) if side == 0 else relay_out(j, c, images))
+
+    def img_copy(j, c, count=per):
+        sl = pl.ds(c * per, count)
         return pltpu.make_async_remote_copy(
             src_ref=send_img.at[j, sl],
             dst_ref=img.at[j, sl],
@@ -91,8 +162,8 @@
             device_id_type=MESH,
         )
 
-    def scl_copy(j, c):
-        sl = pl.ds(c * per, per)
+    def scl_copy(j, c, count=per):
+        sl = pl.ds(c * per, count)
         return pltpu.make_async_remote_copy(
             src_ref=send_scl.at[j, sl],
             dst_ref=rec.at[j, sl],
@@ -148,10 +219,7 @@
 
     def forward(j, c):
         if j < ITERS - 1:
-
-            @pl.when(me > 0)
-            def _():
-                scl_copy(j, c).start()
+            each_copy(j, c, False, 0, lambda copy: copy.start())
 
         @pl.when(me < sections - 1)
         def _():
@@ -159,7 +227,8 @@
                 send_img[j, pl.ds(c * per, per), :, pl.ds(pl.multiple_of(g * LANES, LANES), LANES)] = out
 
             conv(wfh, wfl, write)
-            img_copy(j, c).start()
+
+        each_copy(j, c, True, 0, lambda copy: copy.start())
 
     def fold(val):
         acc = val[:, :LANES]
@@ -175,17 +244,13 @@
 
     def apply(j, c):
         last = j == ITERS - 1
-
-        @pl.when(me > 0)
-        def _():
-            img_copy(j, c).wait_recv()
-
+        pass_on(j, c)
+        each_copy(j, c, True, 1, lambda copy: copy.wait_recv())
         if not last:
+            each_copy(j, c, False, 1, lambda copy: copy.wait_recv())
 
             @pl.when(me < sections - 1)
             def _():
-                scl_copy(j, c).wait_recv()
-
                 def shift_one(s, carry):
                     val = rec[j, c * per + s]
                     if j > 0:
@@ -445,17 +510,18 @@
 
         lax.fori_loop(0, per, final, 0)
 
-    @pl.when(me < sections - 1)
-    def _():
-        for j in range(ITERS):
-            for c in range(CHUNKS):
-                img_copy(j, c).wait_send()
-
-    @pl.when(me > 0)
-    def _():
-        for j in range(ITERS - 1):
-            for c in range(CHUNKS):
-                scl_copy(j, c).wait_send()
+    for j in range(ITERS):
+        for c in range(CHUNKS):
+            each_copy(j, c, True, 0, lambda copy: copy.wait_send())
+            if j < ITERS - 1:
+                each_copy(j, c, False, 0, lambda copy: copy.wait_send())
+            if relayed:
+                for images, via in ((True, img_via), (False, scl_via)):
+                    if images or j < ITERS - 1:
+
+                        @pl.when(me == via)
+                        def _():
+                            relay_out(j, c, images).wait_send()
 
 
 def body(start_lead, start_field, diag_dual, coupling_dual, linear_table, labels, bias_dual, kernels):
@@ -498,6 +564,11 @@
             dma((ITERS - 1, CHUNKS)),
             dma((2, CHUNKS, sections)),
             dma((2, CHUNKS, sections)),
+            pltpu.VMEM((ITERS, specs // 2, rows, width), f32),
+            dma((ITERS, CHUNKS)),
+            dma((ITERS, CHUNKS)),
+            dma((ITERS, CHUNKS)),
+            dma((ITERS, CHUNKS)),
         ],
         compiler_params=pltpu.CompilerParams(collective_id=0, has_side_effects=True, vmem_limit_bytes=56 * 1024 * 1024),
     )(

time: 108 us -> 96.3 us (0.89)
  Pallas kernels: 97.6 us -> 86.3 us
    pallas_call x1, Pallas kernels: 97.6 us -> 86.3 us  [body(): pl.pallas_call(functools.partial(kernel_body, sections, float(unit_count)...]
where the time goes in v2:
time: 96.3 us; the launch traced here: 96.1 us
  Pallas kernels  86.3 us (90%)
  local copies, waits for them, and re-layouts  9.1 us (9%)
    pallas_call x1, Pallas kernels, body(): pl.pallas_call(functools.partial(kernel_body, sections, float(unit_count)...  86.3 us
    unnamed x11, local copies, waits for them, and re-layouts  6.27 us

profile of v2, /device:TPU:0, one launch (start us, length us, event | category | flops | bytes accessed | tf_op | source)
XLA Modules:
  0.0 96.1 jit_solution(4488620685867932736)
XLA Ops:
  0.6 0.0 copy-start.2
  0.6 0.6 copy-done.2
  1.3 0.7 copy.18.lead0
  2.0 0.0 copy-start.3
  2.0 0.7 copy-done.3
  2.6 0.7 copy.19.bias
  3.3 86.3 %shard_map.119 = (f32[16,16,1024]{2,1,0:T(8,128)}, f32[16,16,1024]{2,1,0:T(8,128)}, f32[16,16,1024]{2,1,0:T(8,128)}, f32[16,128]{1,0:T(8,128)}) custom-call(s32[16]{0:T(128)} %labels.1, f32[16,1]{1,0:T(8,128)} %copy.18.lead0, f32[16,16,1024]{2,1,0:T(8,128)} %bitcast.19, f32[16,16,1024]{2,1,0:T(8,128)} %bitcast.20, f32[16,16,1024]{2,1,0:T(8,128)} %bitcast.21, ...), custom_call_target="tpu_custom_call" | custom-call | tf_op jit(solution)/shard_map/pallas_call | solution.py:537
  89.6 1.5 %slice_reduce_fusion = (f32[16]{0:T(128)}, f32[16]{0:T(128)}) fusion(f32[16,128]{1,0:T(8,128)} %get-tuple-element.12), kind=kLoop, calls=%fused_computation | loop fusion | bytes 256 | tf_op jit(solution)/shard_map/slice | solution.py:585
  91.1 0.0 copy-start.1
  91.1 2.4 %copy.26 = f32[16,1,16,1024]{3,2,1,0:T(8,128)} copy(f32[16,1,16,1024]{3,2,1,0:T(8,128)} %bitcast.18) | data formatting | bytes 2097152
  93.5 0.0 copy-done.1
  93.5 0.0 copy-start
  93.5 1.0 %copy.27 = f32[16,1,16,1024]{3,2,1,0:T(8,128)} copy(f32[16,1,16,1024]{3,2,1,0:T(8,128)S(1)} %bitcast.17) | data formatting | bytes 2097152
  94.5 0.6 copy-done
  95.1 1.0 %copy.28 = f32[16,1,16,1024]{3,2,1,0:T(8,128)} copy(f32[16,1,16,1024]{3,2,1,0:T(8,128)S(1)} %bitcast.16) | data formatting | bytes 2097152
Async XLA Ops:
  0.6 0.7 copy-start.2
  2.0 0.7 copy-start.3
  91.1 2.4 %copy-start.1 = (f32[16,16,1024]{2,1,0:T(8,128)S(1)}, f32[16,16,1024]{2,1,0:T(8,128)}, u32[]{:S(2)}) copy-start(f32[16,16,1024]{2,1,0:T(8,128)} %get-tuple-element.10) | copy-start | bytes 3145732
  93.5 1.6 %copy-start = (f32[16,16,1024]{2,1,0:T(8,128)S(1)}, f32[16,16,1024]{2,1,0:T(8,128)}, u32[]{:S(2)}) copy-start(f32[16,16,1024]{2,1,0:T(8,128)} %get-tuple-element.11) | copy-start | bytes 3145732
